TPU v7x, 32 devices: a whole 2x2x4 slice. The times are simulated.
32 devices in a mesh: aa: 4 (over z), ba: 8 (over y, x, core).
Axes of the slice: x: 2, y: 2, z: 4, core: 2. Of those that a mesh axis runs over, the one named last changes fastest.
Arguments:
- feats: bfloat16 [4, 32, 128, 256], P('aa', 'ba'), may hold values from -6 to 6
- conv_one: bfloat16 [3, 3, 3, 256, 256], replicated, may hold values from -0.078125 to 0.078125
- bias_one: float32 [256], replicated, may hold values from -3 to 3
- conv_two: bfloat16 [3, 3, 3, 256, 256], replicated, may hold values from -0.078125 to 0.078125
- bias_two: float32 [256], replicated, may hold values from -3 to 3
- patch_weight: bfloat16 [2, 2, 256, 128], replicated, may hold values from -0.1875 to 0.1875
- patch_bias: float32 [128], replicated, may hold values from -3 to 3
- embed_weight: bfloat16 [128, 2048], replicated, may hold values from -0.5 to 0.5
- embed_bias: float32 [2048], replicated, may hold values from -6 to 6
- norm_gain: float32 [2048], replicated, may hold values from 0.1 to 1.9
- w_query: bfloat16 [2048, 2048], P(None, 'ba'), may hold values from -2 to 2
- w_key: bfloat16 [2048, 2048], P(None, 'ba'), may hold values from -2 to 2
- w_value: bfloat16 [2048, 2048], P(None, 'ba'), may hold values from -0.125 to 0.125
- w_velocity: bfloat16 [2048, 128], P('ba'), may hold values from -0.5 to 0.5
Outputs:
- velocity: float32 [4096, 128], P(('aa', 'ba'))
All inputs are finite; a program needn't handle non-finite values.
Results may differ from a plain program's by a relative error of at most 0.035.
Values may be sent and summed in bfloat16 or wider, within the bound.
A program may use at most 128 MiB of HBM per device.

v0:
```python
import math

import jax
import jax.numpy as jnp
from jax import lax
from jax.sharding import PartitionSpec as P

HEAD_DIM = 64


def with_halo(cells, sides, width):
    for axis, dim in sides:
        count = lax.axis_size(axis)
        ends = count - 1
        head = lax.slice_in_dim(cells, 0, width, axis=dim)
        tail = lax.slice_in_dim(cells, cells.shape[dim] - width, cells.shape[dim], axis=dim)
        cells = jnp.concatenate(
            [
                lax.ppermute(tail, axis, [(i, (i + 1) % count) for i in range(ends)]),
                cells,
                lax.ppermute(head, axis, [((i + 1) % count, i) for i in range(ends)]),
            ],
            axis=dim,
        )
    return cells


def convolve(field, kernel, bias):
    frames, rows, width, chans = field.shape
    padded = with_halo(field, (("aa", 0), ("ba", 1)), 1)
    padded = jnp.pad(padded, ((0, 0), (0, 0), (1, 1), (0, 0)))
    total = jnp.zeros((frames * rows * width, kernel.shape[-1]), jnp.float32)
    for shift_t in range(3):
        for shift_r in range(3):
            window = padded[shift_t : shift_t + frames, shift_r : shift_r + rows]
            stacked = jnp.concatenate(
                [window[:, :, shift_w : shift_w + width] for shift_w in range(3)], axis=-1
            )
            total = total + jnp.dot(
                stacked.reshape(-1, 3 * chans),
                kernel[shift_t, shift_r].reshape(3 * chans, -1),
                preferred_element_type=jnp.float32,
            )
    return (total + bias).reshape(frames, rows, width, -1)


def patchify(field, weight, bias):
    frames, rows, width, chans = field.shape
    blocks = (
        field.reshape(frames, rows // 2, 2, width // 2, 2, chans)
        .transpose(0, 1, 3, 2, 4, 5)
        .reshape(-1, 4 * chans)
    )
    return (
        jnp.dot(blocks, weight.reshape(4 * chans, -1), preferred_element_type=jnp.float32) + bias
    ).astype(jnp.bfloat16)


def normalize(latent_rows, embed_weight, embed_bias, norm_gain):
    hidden = jnp.dot(latent_rows, embed_weight, preferred_element_type=jnp.float32) + embed_bias
    center = hidden - hidden.mean(-1, keepdims=True)
    spread = (center * center).mean(-1, keepdims=True)
    return (center * lax.rsqrt(spread + 1e-05) * norm_gain).astype(jnp.bfloat16)


def attend(queries, keys, values):
    rows, width = queries.shape
    heads = width // HEAD_DIM
    scale = HEAD_DIM ** (-0.5)
    query_heads = queries.reshape(rows, heads, HEAD_DIM)
    start_state = (
        jnp.full((heads, rows), -jnp.inf, jnp.float32),
        jnp.zeros((heads, rows), jnp.float32),
        jnp.zeros((rows, heads, HEAD_DIM), jnp.float32),
    )
    key_rows = lax.all_gather(keys, "aa", axis=0, tiled=True)
    value_rows = lax.all_gather(values, "aa", axis=0, tiled=True)
    count = key_rows.shape[0]
    block = math.gcd(count, 1024)

    def one_step(index, state):
        best, denom, accum = state
        key_block = lax.dynamic_slice_in_dim(key_rows, index * block, block, 0).reshape(
            block, heads, HEAD_DIM
        )
        value_block = lax.dynamic_slice_in_dim(value_rows, index * block, block, 0).reshape(
            block, heads, HEAD_DIM
        )
        scores = (
            jnp.einsum("qhd,khd->hqk", query_heads, key_block, preferred_element_type=jnp.float32)
            * scale
        )
        peak = jnp.maximum(best, scores.max(-1))
        probs = jnp.exp(scores - peak[..., None])
        fade = jnp.exp(best - peak)
        denom = denom * fade + probs.sum(-1)
        accum = accum * fade.T[..., None] + jnp.einsum(
            "hqk,khd->qhd",
            probs.astype(jnp.bfloat16),
            value_block,
            preferred_element_type=jnp.float32,
        )
        return (peak, denom, accum)

    best, denom, accum = lax.fori_loop(0, count // block, one_step, start_state)
    return (accum / denom.T[..., None]).reshape(rows, width).astype(jnp.bfloat16)


def on_device(
    feats,
    conv_one,
    bias_one,
    conv_two,
    bias_two,
    patch_weight,
    patch_bias,
    embed_weight,
    embed_bias,
    norm_gain,
    w_query,
    w_key,
    w_value,
    w_velocity,
):
    first = jax.nn.gelu(convolve(feats, conv_one, bias_one), approximate=False).astype(jnp.bfloat16)
    second = (
        first.astype(jnp.float32)
        + jax.nn.gelu(convolve(first, conv_two, bias_two), approximate=False)
    ).astype(jnp.bfloat16)
    latents = patchify(second, patch_weight, patch_bias)
    width = w_query.shape[1]
    w_joined = jnp.concatenate([w_query, w_key, w_value], axis=1)
    joined = jnp.dot(
        normalize(
            lax.all_gather(latents, "ba", axis=0, tiled=True), embed_weight, embed_bias, norm_gain
        ),
        w_joined,
        preferred_element_type=jnp.float32,
    ).astype(jnp.bfloat16)
    attended = attend(joined[:, :width], joined[:, width : 2 * width], joined[:, 2 * width :])
    return lax.psum_scatter(
        jnp.dot(attended, w_velocity, preferred_element_type=jnp.float32).astype(jnp.bfloat16),
        "ba",
        scatter_dimension=0,
        tiled=True,
    ).astype(jnp.float32)


def solution(mesh):
    return jax.shard_map(
        on_device,
        mesh=mesh,
        in_specs=(
            P("aa", "ba", None, None),
            P(),
            P(),
            P(),
            P(),
            P(),
            P(),
            P(),
            P(),
            P(),
            P(None, "ba"),
            P(None, "ba"),
            P(None, "ba"),
            P("ba", None),
        ),
        out_specs=P(("aa", "ba"), None),
        check_vma=False,
    )
```

profile of v0, /device:TPU:0, one launch (start us, length us, event | category | flops | bytes accessed | tf_op | source)
XLA Modules:
  0.0 332.6 jit_solution(549942878547130094)
XLA Ops:
  6.5 5.1 %collective-permute-start = (bf16[1,4,128,256]{3,2,1,0:T(8,128)(2,1)}, bf16[1,4,128,256]{3,2,1,0:T(8,128)(2,1)S(1)}, u32[]{:S(2)}, u32[]{:S(2)}) collective-permute-start(bf16[1,4,128,256]{3,2,1,0:T(8,128)(2,1)} %param.16), channel_id=1, source_target_pairs={{0,8},{8,16},{16,24},{1,9},{9,17},{17,25},{2,10},{10,18},{18,26},{... | collective-permute-start | bytes 786440 | tf_op jit(solution)/shard_map/ppermute | solution.py:19
  12.9 4.5 %collective-permute-done = bf16[1,4,128,256]{3,2,1,0:T(8,128)(2,1)S(1)} collective-permute-done((bf16[1,4,128,256]{3,2,1,0:T(8,128)(2,1)}, bf16[1,4,128,256]{3,2,1,0:T(8,128)(2,1)S(1)}, u32[]{:S(2)}, u32[]{:S(2)}) %collective-permute-start) | collective-permute-done | bytes 262176 | tf_op jit(solution)/shard_map/ppermute | solution.py:19
  18.5 3.0 collective-permute-done.1
  24.2 2.2 fusion.102
  26.4 1.6 collective-permute-done.3
  33.6 2.1 fusion.69
  36.8 3.5 %collective-permute-start.4 = (bf16[1,4,128,256]{3,2,1,0:T(8,128)(2,1)S(1)}, bf16[1,4,128,256]{3,2,1,0:T(8,128)(2,1)S(1)}, u32[]{:S(2)}, u32[]{:S(2)}) collective-permute-start(bf16[1,4,128,256]{3,2,1,0:T(8,128)(2,1)S(1)} %fusion.66), channel_id=1, source_target_pairs={{0,8},{8,16},{16,24},{1,9},{9,17},{17,25},{2,10},{10,18},{18,26},{... | collective-permute-start | bytes 786440 | tf_op jit(solution)/shard_map/ppermute | solution.py:19
  41.6 2.6 collective-permute-done.4
  44.1 4.4 %collective-permute-done.5 = bf16[1,4,128,256]{3,2,1,0:T(8,128)(2,1)S(1)} collective-permute-done((bf16[1,4,128,256]{3,2,1,0:T(8,128)(2,1)S(1)}, bf16[1,4,128,256]{3,2,1,0:T(8,128)(2,1)S(1)}, u32[]{:S(2)}, u32[]{:S(2)}) %collective-permute-start.5) | collective-permute-done | bytes 262176 | tf_op jit(solution)/shard_map/ppermute | solution.py:21
  49.3 5.3 %collective-permute-start.6 = (bf16[3,1,128,256]{3,2,1,0:T(8,128)(2,1)}, bf16[3,1,128,256]{3,2,1,0:T(8,128)(2,1)}, u32[]{:S(2)}, u32[]{:S(2)}) collective-permute-start(bf16[3,1,128,256]{3,2,1,0:T(8,128)(2,1)} %get-tuple-element.246), channel_id=1, source_target_pairs={{0,1},{1,2},{2,3},{3,4},{4,5},{5,6},{6,7},{8,9},{9,10},{10,11},{11... | collective-permute-start | bytes 589832 | tf_op jit(solution)/shard_map/ppermute | solution.py:19
  54.6 1.5 collective-permute-start.7
  56.1 1.7 fusion.101
  59.6 1.5 select_maximum_fusion.1
  70.8 2.2 fusion.98
  74.7 15.0 %all_gather.9 = bf16[1024,128]{1,0:T(8,128)(2,1)S(1)} all-gather(bf16[128,128]{1,0:T(8,128)(2,1)S(1)} %fusion.31), channel_id=1, replica_groups=mesh['aa'=4,'ba'=8] {'ba'}, dimensions={0}, use_global_device_ids=true | all-gather | bytes 294912 | tf_op jit(solution)/shard_map/all_gather | solution.py:135
  92.9 4.3 %fusion.25 = bf16[1024,768]{0,1:T(8,128)(2,1)S(1)} fusion(bf16[2048,256]{1,0:T(8,128)(2,1)S(1)} %copy-done.16, bf16[2048,256]{1,0:T(8,128)(2,1)S(1)} %copy-done.17, bf16[2048,256]{1,0:T(8,128)(2,1)S(1)} %copy-done.18, f32[1024,2048]{1,0:T(8,128)S(1)} %get-tuple-element.255, f32[2048]{0:T(1024)S(1)} %copy-done.19, f32[1024]{0:T(1024)S(1)} %add_rsqrt_fusion, ...), kind=kOutput, calls=%fused_computation.33 | convolution fusion | flops 3241934848 | bytes 13131776 | tf_op jit(solution)/shard_map/dot_general | solution.py:133
  99.4 43.0 %all-gather.3.cloned.1.call-done = bf16[4096,256]{0,1:T(8,128)(2,1)} async-done(((bf16[1024,256]{0,1:T(8,128)(2,1)}), bf16[4096,256]{0,1:T(8,128)(2,1)}) %all-gather.3.cloned.1.call-update) | async-done | bytes 2097168 | tf_op jit(solution)/shard_map/all_gather | solution.py:76
  142.4 46.1 %all-gather.5.cloned.1.call-done = bf16[4096,256]{0,1:T(8,128)(2,1)} async-done(((bf16[1024,256]{0,1:T(8,128)(2,1)}), bf16[4096,256]{0,1:T(8,128)(2,1)}) %all-gather.5.cloned.1.call-update) | async-done | bytes 2097168 | tf_op jit(solution)/shard_map/all_gather | solution.py:77
  188.4 101.7 %while.18 = (s32[]{:T(128)}, f32[4,1024]{1,0:T(4,128)S(1)}, f32[4,1024]{1,0:T(4,128)S(1)}, f32[1024,4,64]{0,2,1:T(8,128)S(1)}, bf16[4096,256]{0,1:T(8,128)(2,1)}...) while((s32[]{:T(128)}, f32[4,1024]{1,0:T(4,128)S(1)}, ...), condition=%wide.region_5.6_spmd.clone, body=%wide.region_2.5_spmd.clone.sunk | while | flops 1108107264 | bytes 56361128 | solution.py:105
  189.7 8.1 %bitcast_reduce_fusion.2 = (f32[4,1024]{1,0:T(4,128)S(1)}, f32[4,1024,1024]{2,1,0:T(8,128)}) fusion(bf16[1024,4,64]{0,2,1:T(8,128)(2,1)S(1)} %bitcast.131, bf16[1024,4,64]{0,2,1:T(8,128)(2,1)S(1)} %get-tuple-element.340), kind=kOutput, calls=%fused_computation.1.clone.1 | convolution fusion | flops 545255424 | bytes 17842176 | tf_op jit(solution)/shard_map/while/body/eval_jaxpr/qhd,khd->hqk/dot_general | solution.py:90
  197.9 7.4 %fusion.168 = f32[1024,4,64]{0,2,1:T(8,128)S(1)} fusion(bf16[1024,4,64]{0,2,1:T(8,128)(2,1)S(1)} %bitcast.132, f32[4,1024,1024]{2,1,0:T(8,128)} %get-tuple-element.310, f32[4,1024]{1,0:T(4,128)S(1)} %get-tuple-element.336, f32[1024,4,64]{0,2,1:T(8,128)S(1)} %get-tuple-element.327, f32[1024,4]{0,1:T(4,128)S(1)} %get-tuple-element.312, pred[]{:T(512)S(6)} %compare.43), kind=kOutput, calls=%fused_computation.7.clone.1 | convolution fusion | flops 550240256 | bytes 19431424 | tf_op jit(solution)/shard_map/while/body/eval_jaxpr/hqk,khd->qhd/dot_general | solution.py:97
  205.2 8.5 %fusion.166 = f32[4,1024]{1,0:T(4,128)S(1)} fusion(f32[4,1024,1024]{2,1,0:T(8,128)} %get-tuple-element.310, f32[4,1024]{1,0:T(4,128)S(1)} %get-tuple-element.336), kind=kLoop, calls=%fused_computation.4.clone.1 | loop fusion | flops 12578816 | bytes 16809984 | tf_op jit(solution)/shard_map/while/body/eval_jaxpr/reduce_sum | solution.py:96
  215.1 8.1 %bitcast_reduce_fusion.2 = (f32[4,1024]{1,0:T(4,128)S(1)}, f32[4,1024,1024]{2,1,0:T(8,128)}) fusion(bf16[1024,4,64]{0,2,1:T(8,128)(2,1)S(1)} %bitcast.131, bf16[1024,4,64]{0,2,1:T(8,128)(2,1)S(1)} %get-tuple-element.340), kind=kOutput, calls=%fused_computation.1.clone.1 | convolution fusion | flops 545255424 | bytes 17842176 | tf_op jit(solution)/shard_map/while/body/eval_jaxpr/qhd,khd->hqk/dot_general | solution.py:90
  223.3 7.4 %fusion.168 = f32[1024,4,64]{0,2,1:T(8,128)S(1)} fusion(bf16[1024,4,64]{0,2,1:T(8,128)(2,1)S(1)} %bitcast.132, f32[4,1024,1024]{2,1,0:T(8,128)} %get-tuple-element.310, f32[4,1024]{1,0:T(4,128)S(1)} %get-tuple-element.336, f32[1024,4,64]{0,2,1:T(8,128)S(1)} %get-tuple-element.327, f32[1024,4]{0,1:T(4,128)S(1)} %get-tuple-element.312, pred[]{:T(512)S(6)} %compare.43), kind=kOutput, calls=%fused_computation.7.clone.1 | convolution fusion | flops 550240256 | bytes 19431424 | tf_op jit(solution)/shard_map/while/body/eval_jaxpr/hqk,khd->qhd/dot_general | solution.py:97
  230.7 8.5 %fusion.166 = f32[4,1024]{1,0:T(4,128)S(1)} fusion(f32[4,1024,1024]{2,1,0:T(8,128)} %get-tuple-element.310, f32[4,1024]{1,0:T(4,128)S(1)} %get-tuple-element.336), kind=kLoop, calls=%fused_computation.4.clone.1 | loop fusion | flops 12578816 | bytes 16809984 | tf_op jit(solution)/shard_map/while/body/eval_jaxpr/reduce_sum | solution.py:96
  240.5 8.1 %bitcast_reduce_fusion.2 = (f32[4,1024]{1,0:T(4,128)S(1)}, f32[4,1024,1024]{2,1,0:T(8,128)}) fusion(bf16[1024,4,64]{0,2,1:T(8,128)(2,1)S(1)} %bitcast.131, bf16[1024,4,64]{0,2,1:T(8,128)(2,1)S(1)} %get-tuple-element.340), kind=kOutput, calls=%fused_computation.1.clone.1 | convolution fusion | flops 545255424 | bytes 17842176 | tf_op jit(solution)/shard_map/while/body/eval_jaxpr/qhd,khd->hqk/dot_general | solution.py:90
  248.7 7.4 %fusion.168 = f32[1024,4,64]{0,2,1:T(8,128)S(1)} fusion(bf16[1024,4,64]{0,2,1:T(8,128)(2,1)S(1)} %bitcast.132, f32[4,1024,1024]{2,1,0:T(8,128)} %get-tuple-element.310, f32[4,1024]{1,0:T(4,128)S(1)} %get-tuple-element.336, f32[1024,4,64]{0,2,1:T(8,128)S(1)} %get-tuple-element.327, f32[1024,4]{0,1:T(4,128)S(1)} %get-tuple-element.312, pred[]{:T(512)S(6)} %compare.43), kind=kOutput, calls=%fused_computation.7.clone.1 | convolution fusion | flops 550240256 | bytes 19431424 | tf_op jit(solution)/shard_map/while/body/eval_jaxpr/hqk,khd->qhd/dot_general | solution.py:97
  256.1 8.5 %fusion.166 = f32[4,1024]{1,0:T(4,128)S(1)} fusion(f32[4,1024,1024]{2,1,0:T(8,128)} %get-tuple-element.310, f32[4,1024]{1,0:T(4,128)S(1)} %get-tuple-element.336), kind=kLoop, calls=%fused_computation.4.clone.1 | loop fusion | flops 12578816 | bytes 16809984 | tf_op jit(solution)/shard_map/while/body/eval_jaxpr/reduce_sum | solution.py:96
  266.0 8.1 %bitcast_reduce_fusion.2 = (f32[4,1024]{1,0:T(4,128)S(1)}, f32[4,1024,1024]{2,1,0:T(8,128)}) fusion(bf16[1024,4,64]{0,2,1:T(8,128)(2,1)S(1)} %bitcast.131, bf16[1024,4,64]{0,2,1:T(8,128)(2,1)S(1)} %get-tuple-element.340), kind=kOutput, calls=%fused_computation.1.clone.1 | convolution fusion | flops 545255424 | bytes 17842176 | tf_op jit(solution)/shard_map/while/body/eval_jaxpr/qhd,khd->hqk/dot_general | solution.py:90
  274.1 7.4 %fusion.168 = f32[1024,4,64]{0,2,1:T(8,128)S(1)} fusion(bf16[1024,4,64]{0,2,1:T(8,128)(2,1)S(1)} %bitcast.132, f32[4,1024,1024]{2,1,0:T(8,128)} %get-tuple-element.310, f32[4,1024]{1,0:T(4,128)S(1)} %get-tuple-element.336, f32[1024,4,64]{0,2,1:T(8,128)S(1)} %get-tuple-element.327, f32[1024,4]{0,1:T(4,128)S(1)} %get-tuple-element.312, pred[]{:T(512)S(6)} %compare.43), kind=kOutput, calls=%fused_computation.7.clone.1 | convolution fusion | flops 550240256 | bytes 19431424 | tf_op jit(solution)/shard_map/while/body/eval_jaxpr/hqk,khd->qhd/dot_general | solution.py:97
  281.5 8.5 %fusion.166 = f32[4,1024]{1,0:T(4,128)S(1)} fusion(f32[4,1024,1024]{2,1,0:T(8,128)} %get-tuple-element.310, f32[4,1024]{1,0:T(4,128)S(1)} %get-tuple-element.336), kind=kLoop, calls=%fused_computation.4.clone.1 | loop fusion | flops 12578816 | bytes 16809984 | tf_op jit(solution)/shard_map/while/body/eval_jaxpr/reduce_sum | solution.py:96
  292.0 32.6 %reduce-scatter.2.cloned.1.call-done = bf16[128,128]{1,0:T(8,128)(2,1)} async-done(((bf16[1024,128]{1,0:T(8,128)(2,1)}), bf16[128,128]{1,0:T(8,128)(2,1)}) %reduce-scatter.2.cloned.1.call-update) | async-done | bytes 32784 | tf_op jit(solution)/shard_map/reduce_scatter | solution.py:141
  (124 shorter events, 40.4 us)
Async XLA Ops:
  6.5 83.1 %copy-start = (bf16[128,2048]{1,0:T(8,128)(2,1)S(1)}, bf16[128,2048]{1,0:T(8,128)(2,1)}, u32[]{:S(2)}) copy-start(bf16[128,2048]{1,0:T(8,128)(2,1)} %param.23) | copy-start | bytes 1572868
  6.5 135.8 %all-gather.3.cloned.1.call-start = ((), (), s32[]{:S(2)}) async-start(), calls=%async_computation.1 | async-start | bytes 2621440 | tf_op jit(solution)/shard_map/all_gather | solution.py:76
  6.5 10.9 %collective-permute-start = (bf16[1,4,128,256]{3,2,1,0:T(8,128)(2,1)}, bf16[1,4,128,256]{3,2,1,0:T(8,128)(2,1)S(1)}, u32[]{:S(2)}, u32[]{:S(2)}) collective-permute-start(bf16[1,4,128,256]{3,2,1,0:T(8,128)(2,1)} %param.16), channel_id=1, source_target_pairs={{0,8},{8,16},{16,24},{1,9},{9,17},{17,25},{2,10},{10,18},{18,26},{... | collective-permute-start | bytes 786440 | tf_op jit(solution)/shard_map/ppermute | solution.py:19
  11.6 9.9 %collective-permute-start.1 = (bf16[1,4,128,256]{3,2,1,0:T(8,128)(2,1)}, bf16[1,4,128,256]{3,2,1,0:T(8,128)(2,1)S(1)}, u32[]{:S(2)}, u32[]{:S(2)}) collective-permute-start(bf16[1,4,128,256]{3,2,1,0:T(8,128)(2,1)} %param.16), channel_id=1, source_target_pairs={{8,0},{16,8},{24,16},{9,1},{17,9},{25,17},{10,2},{18,10},{26,18},{... | collective-permute-start | bytes 786440 | tf_op jit(solution)/shard_map/ppermute | solution.py:21
  21.6 4.8 %collective-permute-start.2 = (bf16[3,1,128,256]{3,2,1,0:T(8,128)(2,1)S(1)}, bf16[3,1,128,256]{3,2,1,0:T(8,128)(2,1)S(1)}, u32[]{:S(2)}, u32[]{:S(2)}) collective-permute-start(bf16[3,1,128,256]{3,2,1,0:T(8,128)(2,1)S(1)} %get-tuple-element.248), channel_id=1, source_target_pairs={{0,1},{1,2},{2,3},{3,4},{4,5},{5,6},{6,7},{8,9},{9,10},{10,11},{11... | collective-permute-start | bytes 589832 | tf_op jit(solution)/shard_map/ppermute | solution.py:19
  22.9 5.1 %collective-permute-start.3 = (bf16[3,1,128,256]{3,2,1,0:T(8,128)(2,1)S(1)}, bf16[3,1,128,256]{3,2,1,0:T(8,128)(2,1)S(1)}, u32[]{:S(2)}, u32[]{:S(2)}) collective-permute-start(bf16[3,1,128,256]{3,2,1,0:T(8,128)(2,1)S(1)} %get-tuple-element.247), channel_id=1, source_target_pairs={{1,0},{2,1},{3,2},{4,3},{5,4},{6,5},{7,6},{9,8},{10,9},{11,10},{12... | collective-permute-start | bytes 589832 | tf_op jit(solution)/shard_map/ppermute | solution.py:21
  28.5 1.0 copy-start.10
  33.6 22.5 %copy-start.2 = (bf16[3,3,3,256,256]{4,3,2,1,0:T(8,128)(2,1)S(1)}, bf16[3,3,3,256,256]{4,3,2,1,0:T(8,128)(2,1)}, u32[]{:S(2)}) copy-start(bf16[3,3,3,256,256]{4,3,2,1,0:T(8,128)(2,1)} %param.19) | copy-start | bytes 10616836
  36.8 7.3 %collective-permute-start.4 = (bf16[1,4,128,256]{3,2,1,0:T(8,128)(2,1)S(1)}, bf16[1,4,128,256]{3,2,1,0:T(8,128)(2,1)S(1)}, u32[]{:S(2)}, u32[]{:S(2)}) collective-permute-start(bf16[1,4,128,256]{3,2,1,0:T(8,128)(2,1)S(1)} %fusion.66), channel_id=1, source_target_pairs={{0,8},{8,16},{16,24},{1,9},{9,17},{17,25},{2,10},{10,18},{18,26},{... | collective-permute-start | bytes 786440 | tf_op jit(solution)/shard_map/ppermute | solution.py:19
  40.3 8.3 %collective-permute-start.5 = (bf16[1,4,128,256]{3,2,1,0:T(8,128)(2,1)S(1)}, bf16[1,4,128,256]{3,2,1,0:T(8,128)(2,1)S(1)}, u32[]{:S(2)}, u32[]{:S(2)}) collective-permute-start(bf16[1,4,128,256]{3,2,1,0:T(8,128)(2,1)S(1)} %fusion.66), channel_id=1, source_target_pairs={{8,0},{16,8},{24,16},{9,1},{17,9},{25,17},{10,2},{18,10},{26,18},{... | collective-permute-start | bytes 786440 | tf_op jit(solution)/shard_map/ppermute | solution.py:21
  49.3 9.1 %collective-permute-start.6 = (bf16[3,1,128,256]{3,2,1,0:T(8,128)(2,1)}, bf16[3,1,128,256]{3,2,1,0:T(8,128)(2,1)}, u32[]{:S(2)}, u32[]{:S(2)}) collective-permute-start(bf16[3,1,128,256]{3,2,1,0:T(8,128)(2,1)} %get-tuple-element.246), channel_id=1, source_target_pairs={{0,1},{1,2},{2,3},{3,4},{4,5},{5,6},{6,7},{8,9},{9,10},{10,11},{11... | collective-permute-start | bytes 589832 | tf_op jit(solution)/shard_map/ppermute | solution.py:19
  54.6 5.0 %collective-permute-start.7 = (bf16[3,1,128,256]{3,2,1,0:T(8,128)(2,1)}, bf16[3,1,128,256]{3,2,1,0:T(8,128)(2,1)S(1)}, u32[]{:S(2)}, u32[]{:S(2)}) collective-permute-start(bf16[3,1,128,256]{3,2,1,0:T(8,128)(2,1)} %get-tuple-element.245), channel_id=1, source_target_pairs={{1,0},{2,1},{3,2},{4,3},{5,4},{6,5},{7,6},{9,8},{10,9},{11,10},{12... | collective-permute-start | bytes 589832 | tf_op jit(solution)/shard_map/ppermute | solution.py:21
  62.0 1.1 copy-start.9
  63.1 1.0 copy-start.8
  64.5 1.0 copy-start.7
  64.8 1.1 copy-start.6
  65.9 1.0 copy-start.11
  65.9 1.1 copy-start.21
  66.3 1.1 copy-start.5
  67.3 1.0 copy-start.4
  68.3 1.0 copy-start.3
  68.7 1.0 copy-start.14
  70.8 2.7 copy-start.15
  70.8 18.9 %copy-start.12 = (f32[2048]{0:T(1024)S(1)}, f32[2048]{0:T(1024)}, u32[]{:S(2)}) copy-start(f32[2048]{0:T(1024)} %param.24) | copy-start | bytes 24580
  91.0 1.3 copy-start.16
  91.0 1.5 copy-start.17
  91.0 1.8 copy-start.18
  91.0 1.8 copy-start.19
  98.3 90.1 %all-gather.5.cloned.1.call-start = ((), (), s32[]{:S(2)}) async-start(), calls=%async_computation.2 | async-start | bytes 2621440 | tf_op jit(solution)/shard_map/all_gather | solution.py:77
  99.1 225.6 %reduce-scatter.2.cloned.1.call-start = ((), (), s32[]{:S(2)}) async-start(), calls=%async_computation.3 | async-start | bytes 294912 | tf_op jit(solution)/shard_map/reduce_scatter | solution.py:141
  290.1 0.8 copy-start.13
  290.1 35.9 %copy-start.1 = (bf16[128,2048]{1,0:T(8,128)(2,1)S(1)}, bf16[128,2048]{1,0:T(8,128)(2,1)}, u32[]{:S(2)}) copy-start(bf16[128,2048]{1,0:T(8,128)(2,1)} %param.23) | copy-start | bytes 1572868
  (1 other events, 0.7 us)
Sparse Core Ops, SparseCore 0:
  98.4 43.8 all-gather.2
  143.9 44.4 all-gather.4
  292.1 32.4 reduce-scatter.1
where the time goes:
time: 334 us; the launch traced here: 333 us
  waiting for transfers between devices  140 us (42%)
  matrix products  78.4 us (23%)
  other arithmetic  45.5 us (14%)
  starting transfers between devices  20.9 us (6%)
  local copies, waits for them, and re-layouts  19.2 us (6%)
  blocking collectives  15 us (4%)
  between operations  13.7 us (4%)
    all_gather x1, waiting for transfers between devices, attend(): value_rows = lax.all_gather(values, 'aa', axis=0, tiled=True)  46.1 us
    all_gather x1, waiting for transfers between devices, attend(): key_rows = lax.all_gather(keys, 'aa', axis=0, tiled=True)  43 us
    reduce_sum x4, other arithmetic, one_step(): denom = denom * fade + probs.sum(-1)  34.1 us
    reduce_scatter x1, waiting for transfers between devices, on_device(): lax.psum_scatter(jnp.dot(attended, w_velocity, preferred_element_type=jnp...  32.6 us
    dot_general x4, matrix products, one_step(): jnp.einsum('qhd,khd->hqk', query_heads, key_block, preferred_element_type...  32.6 us
    dot_general x4, matrix products, one_step(): jnp.einsum('hqk,khd->qhd', probs.astype(jnp.bfloat16), value_block, prefe...  29.5 us
    ppermute x4, starting transfers between devices, with_halo(): lax.ppermute(tail, axis, [(i, (i + 1) % count) for i in range(ends)])  15.2 us
    all_gather x1, blocking collectives, on_device(): lax.all_gather(latents, 'ba', axis=0, tiled=True)  15 us
  transfers between devices with their start and end apart: 11, of which 9 were waited for; matrix products, arithmetic and copies ran while one was open for 2% of the time, Pallas kernels for 0%

commit v1 on v0

v1 whole, which is shorter than its diff:
```python
import functools
import math

import jax
import jax.numpy as jnp
from jax import lax
from jax.experimental import pallas as pl
from jax.experimental.pallas import tpu as pltpu
from jax.sharding import PartitionSpec as P

HEAD_DIM = 64
SLOT = 128
MESH = pl.DeviceIdType.MESH
F32 = jnp.float32
BF16 = jnp.bfloat16
VMEM_BYTES = 60 << 20
DIRECTIONS = ((0, -1), (0, 1), (-1, 0), (1, 0), (-1, -1), (-1, 1), (1, -1), (1, 1))


def dot(left, right):
    return jnp.dot(left, right, preferred_element_type=F32)


def two_parts(value):
    high = value.astype(BF16)
    return high, (value - high.astype(F32)).astype(BF16)


def gelu(value):
    return 0.5 * value * (1.0 + lax.erf(value * (0.5**0.5)))


def encode_kernel(
    n_aa, n_ba,
    feats, conv_one, bias_one, conv_two, bias_two, patch_weight, patch_bias,
    embed_weight, embed_bias, norm_gain, w_query, w_key, w_value,
    gathered, merged, gram,
    field_one, field_two, taps_one, taps_two, w_joined, acc, pair, load_sem,
    send_sem, recv_sem, aa_send, aa_recv, ba_send, ba_recv, core_send, core_recv,
):
    aa, ba = lax.axis_index("aa"), lax.axis_index("ba")
    _, rows, width, chans = feats.shape
    partner = ba + 1 - 2 * (ba % 2)
    half = n_ba // 2
    qwidth = w_query.shape[1]

    loads = [
        pltpu.make_async_copy(feats.at[0], field_one.at[1, pl.ds(1, rows)], load_sem.at[0]),
        pltpu.make_async_copy(conv_one, taps_one, load_sem.at[1]),
        pltpu.make_async_copy(w_query, w_joined.at[0], load_sem.at[2]),
        pltpu.make_async_copy(w_key, w_joined.at[1], load_sem.at[3]),
        pltpu.make_async_copy(w_value, w_joined.at[2], load_sem.at[4]),
        pltpu.make_async_copy(conv_two, taps_two, load_sem.at[5]),
    ]
    for load in loads:
        load.start()

    def there(da, db):
        inside = None
        if da == -1:
            inside = aa > 0
        if da == 1:
            inside = aa < n_aa - 1
        if db == -1:
            inside = ba > 0 if inside is None else jnp.logical_and(inside, ba > 0)
        if db == 1:
            last = ba < n_ba - 1
            inside = last if inside is None else jnp.logical_and(inside, last)
        return inside

    barrier = pltpu.get_barrier_semaphore()
    for da, db in DIRECTIONS:
        @pl.when(there(da, db))
        def _():
            pl.semaphore_signal(barrier, inc=1, device_id=(aa + da, ba + db), device_id_type=MESH)
    for step in range(1, n_aa):
        pl.semaphore_signal(
            barrier, inc=1, device_id=((aa + step) % n_aa, ba), device_id_type=MESH
        )
    for step in range(1, half):
        pl.semaphore_signal(
            barrier, inc=1, device_id=(aa, (ba + 2 * step) % n_ba), device_id_type=MESH
        )
    pl.semaphore_signal(barrier, inc=1, device_id=(aa, partner), device_id_type=MESH)

    def landing(field, da, db):
        row = slice(1, rows + 1) if db == 0 else (slice(0, 1) if db == 1 else slice(rows + 1, rows + 2))
        return field.at[1 - da, row]

    def halo(field, at):
        da, db = DIRECTIONS[at]
        row = slice(1, rows + 1) if db == 0 else (slice(rows, rows + 1) if db == 1 else slice(1, 2))
        return pltpu.make_async_remote_copy(
            src_ref=field.at[1, row],
            dst_ref=landing(field, da, db),
            send_sem=send_sem.at[0 if field is field_one else 1, at],
            recv_sem=recv_sem.at[0 if field is field_one else 1, at],
            device_id=(aa + da, ba + db),
            device_id_type=MESH,
        )

    def each(field, which, act):
        for at in which:
            da, db = DIRECTIONS[at]
            act(field, at, da, db)

    def send(field, at, da, db):
        @pl.when(there(da, db))
        def _():
            halo(field, at).start()

    def arrive(field, at, da, db):
        @pl.when(there(-da, -db))
        def _():
            halo(field, at).wait_recv()

    def sent(field, at, da, db):
        @pl.when(there(da, db))
        def _():
            halo(field, at).wait_send()

    def blank(field, at, da, db):
        @pl.when(jnp.logical_not(there(-da, -db)))
        def _():
            target = landing(field, da, db)
            target[...] = jnp.zeros(target.shape, target.dtype)

    neighbours = jnp.int32(n_aa - 1 + half - 1 + 1)
    for da, db in DIRECTIONS:
        neighbours = neighbours + there(da, db).astype(jnp.int32)
    every = range(8)
    each(field_one, every, blank)
    each(field_two, every, blank)
    pl.semaphore_wait(barrier, neighbours)
    loads[0].wait()
    each(field_one, every, send)

    embed = embed_weight[...].astype(F32)
    centred = jnp.concatenate(
        [
            embed - embed.mean(-1, keepdims=True),
            jnp.broadcast_to(
                embed_bias[...] - embed_bias[...].mean(-1, keepdims=True), (8, embed.shape[1])
            ),
        ],
        axis=0,
    )
    gram[...] = lax.dot_general(
        centred, centred, (((1,), (1,)), ((), ())),
        precision=lax.Precision.HIGHEST, preferred_element_type=F32,
    ) * (1.0 / embed.shape[1])
    gained_high, gained_low = two_parts(centred * norm_gain[...])
    for which in range(3):
        loads[2 + which].wait()
        product = dot(gained_high, w_joined[which]) + dot(gained_low, w_joined[which])
        if which == 0:
            product = product * (HEAD_DIM**-0.5 * math.log2(math.e))
        blanks = jnp.zeros((product.shape[0], SLOT - HEAD_DIM), F32)
        for head in range(qwidth // HEAD_DIM):
            piece = product[:, head * HEAD_DIM : (head + 1) * HEAD_DIM]
            merged[which, :, head * SLOT : (head + 1) * SLOT] = jnp.concatenate(
                [piece, blanks], axis=1
            )

    def convolve(field, taps, bias):
        def tap(shift_t, shift_r, first):
            window = field[shift_t, pl.ds(shift_r, rows)].reshape(rows * width, chans)
            for shift_w in range(3):
                part = dot(window, taps[(shift_t * 3 + shift_r) * 3 + shift_w])
                if first:
                    acc[shift_w] = part
                else:
                    acc[shift_w] += part

        tap(1, 1, True)
        each(field, (0, 1), arrive)
        tap(1, 0, False)
        tap(1, 2, False)
        each(field, (2, 3), arrive)
        tap(0, 1, False)
        tap(2, 1, False)
        each(field, (4, 5, 6, 7), arrive)

        @pl.loop(0, 2)
        def _(index):
            tap(0, 2 * index, False)
            tap(2, 2 * index, False)

        total = acc[1] + bias
        place = lax.broadcasted_iota(jnp.int32, total.shape, 0) % width
        total += jnp.where(place == 0, 0.0, pltpu.roll(acc[0], 1, 0))
        total += jnp.where(place == width - 1, 0.0, pltpu.roll(acc[2], rows * width - 1, 0))
        return total

    loads[1].wait()
    first = gelu(convolve(field_one, taps_one, bias_one[...])).astype(BF16)
    field_two[1, 1 : rows + 1] = first.reshape(rows, width, chans)
    each(field_two, every, send)
    loads[5].wait()
    total = convolve(field_two, taps_two, bias_two[...])
    own = field_two[1, 1 : rows + 1].reshape(rows * width, chans).astype(F32)
    second = (own + gelu(total)).astype(BF16)

    tokens = rows * width // 4
    line = width // 2
    for block in range(rows // 2):
        upper = second[(2 * block) * width : (2 * block + 1) * width]
        lower = second[(2 * block + 1) * width : (2 * block + 2) * width]
        for col in range(2):
            pair[col] = dot(upper, patch_weight[0, col]) + dot(lower, patch_weight[1, col])
        patches = (
            pair[0, pl.ds(0, line, stride=2), :] + pair[1, pl.ds(1, line, stride=2), :]
            + patch_bias[...]
        ).astype(BF16)
        gathered[ba, pl.ds(pl.multiple_of(aa * tokens + block * line, line), line), :] = patches

    def along_aa(step):
        block = gathered.at[ba, pl.ds(pl.multiple_of(aa * tokens, tokens), tokens)]
        return pltpu.make_async_remote_copy(
            src_ref=block, dst_ref=block, send_sem=aa_send.at[step], recv_sem=aa_recv.at[step],
            device_id=((aa + step) % n_aa, ba), device_id_type=MESH,
        )

    def along_ba(step):
        return pltpu.make_async_remote_copy(
            src_ref=gathered.at[ba], dst_ref=gathered.at[ba],
            send_sem=ba_send.at[step], recv_sem=ba_recv.at[step],
            device_id=(aa, (ba + 2 * step) % n_ba), device_id_type=MESH,
        )

    def to_partner(step):
        block = gathered.at[(ba + n_ba - 2 * step) % n_ba]
        return pltpu.make_async_remote_copy(
            src_ref=block, dst_ref=block, send_sem=core_send.at[step], recv_sem=core_recv.at[step],
            device_id=(aa, partner), device_id_type=MESH,
        )

    for step in range(1, n_aa):
        along_aa(step).start()
    each(field_one, every, sent)
    each(field_two, every, sent)
    for step in range(1, n_aa):
        along_aa(step).wait_recv()
    for step in range(1, half):
        along_ba(step).start()
    to_partner(0).start()
    for step in range(1, half):
        along_ba(step).wait_recv()
        to_partner(step).start()
    for step in range(half):
        to_partner(step).wait_recv()
    for step in range(1, n_aa):
        along_aa(step).wait_send()
    for step in range(1, half):
        along_ba(step).wait_send()
    for step in range(half):
        to_partner(step).wait_send()


def attend_kernel(
    n_aa, n_ba, span, chunk,
    gathered, merged, gram, w_velocity, out,
    queries, keys, values, split, shares, arrived, send_sem, recv_sem,
):
    aa, ba = lax.axis_index("aa"), lax.axis_index("ba")
    heads = w_velocity.shape[0] // HEAD_DIM
    count = gathered.shape[1] // n_aa
    lat = gathered.shape[2]
    per_span = span // count

    barrier = pltpu.get_barrier_semaphore()
    for step in range(1, n_ba):
        pl.semaphore_signal(
            barrier, inc=1, device_id=(aa, (ba + step) % n_ba), device_id_type=MESH
        )

    for which in range(3):
        high, low = two_parts(merged[which, :lat])
        split[which, 0] = high
        split[which, 1] = low
    gram_high, gram_low = two_parts(gram[:lat, :lat])
    slope = 2.0 * gram[lat : lat + 1, :lat]
    floor = gram[lat : lat + 1, lat : lat + 1]

    def spread_of(latents):
        bent = dot(latents, gram_high) + dot(latents, gram_low) + slope
        power = (bent * latents.astype(F32)).sum(-1, keepdims=True) + floor
        return lax.rsqrt(jnp.maximum(power, 0.0) + 1e-05)

    def project(latents, scale, which):
        flat = dot(latents, split[which, 0]) + dot(latents, split[which, 1])
        return ((flat + merged[which, lat : lat + 1]) * scale).astype(BF16)

    column = lax.broadcasted_iota(jnp.int32, (gathered.shape[1], SLOT), 1)

    @pl.loop(0, n_ba)
    def _(block):
        latents = gathered[block]
        scale = spread_of(latents)
        projected_keys = project(latents, scale, 1)
        projected_values = project(latents, scale, 2)
        where = pl.ds(pl.multiple_of(block * latents.shape[0], latents.shape[0]), latents.shape[0])
        for head in range(heads):
            keys[head, where] = projected_keys[:, head * SLOT : (head + 1) * SLOT]
            values[head, where] = jnp.where(
                column == HEAD_DIM,
                jnp.ones((), BF16),
                projected_values[:, head * SLOT : (head + 1) * SLOT],
            )
        mine = gathered[block, pl.ds(pl.multiple_of(aa * count, count), count)]
        asked = project(mine, spread_of(mine), 0)
        there = pl.ds(pl.multiple_of(block * count, count), count)
        for head in range(heads):
            queries[head, there] = asked[:, head * SLOT : (head + 1) * SLOT]

    pl.semaphore_wait(barrier, n_ba - 1)

    def share(dest):
        offset = (dest + n_ba - ba) % n_ba
        return pltpu.make_async_remote_copy(
            src_ref=shares.at[dest], dst_ref=arrived.at[ba],
            send_sem=send_sem.at[offset], recv_sem=recv_sem.at[offset],
            device_id=(aa, dest), device_id_type=MESH,
        )

    spans = n_ba // per_span
    total = keys.shape[1]
    big = math.gcd(total, 4096)

    @pl.loop(0, spans)
    def _(step):
        at = (ba // per_span + 1 + step) % spans
        where = pl.ds(pl.multiple_of(at * span, span), span)

        def one_head(head, velocity):
            asked = queries[head, where]

            def one_big(index, state):
                best, accum = state
                for piece in range(big // chunk):
                    held = pl.ds(pl.multiple_of(index * big + piece * chunk, chunk), chunk)
                    scores = lax.dot_general(
                        asked, keys[head, held], (((1,), (1,)), ((), ())),
                        preferred_element_type=F32,
                    )
                    peak = jnp.maximum(best, scores.max(-1, keepdims=True))
                    probs = jnp.exp2(scores - peak).astype(BF16)
                    accum = accum * jnp.exp2(best - peak) + dot(probs, values[head, held])
                    best = peak
                return best, accum

            state = (jnp.full((span, 1), -jnp.inf, F32), jnp.zeros((span, SLOT), F32))
            if total == big:
                _, accum = one_big(0, state)
            else:
                _, accum = lax.fori_loop(0, total // big, one_big, state)
            attended = (accum[:, :HEAD_DIM] / accum[:, HEAD_DIM : HEAD_DIM + 1]).astype(BF16)
            rows = pl.ds(pl.multiple_of(head * HEAD_DIM, HEAD_DIM), HEAD_DIM)
            return velocity + dot(attended, w_velocity[rows])

        velocity = lax.fori_loop(0, heads, one_head, jnp.zeros((span, w_velocity.shape[1]), F32))
        for part in range(per_span):
            dest = at * per_span + part
            shares[dest] = velocity[part * count : (part + 1) * count].astype(BF16)

            @pl.when(dest != ba)
            def _():
                share(dest).start()

    summed = shares[ba].astype(F32)
    for offset in range(1, n_ba):
        share((ba + offset) % n_ba).wait_recv()
        summed += arrived[(ba + n_ba - offset) % n_ba].astype(F32)
    out[...] = summed
    for offset in range(1, n_ba):
        share((ba + offset) % n_ba).wait_send()


def on_device(
    n_aa, n_ba,
    feats, conv_one, bias_one, conv_two, bias_two, patch_weight, patch_bias,
    embed_weight, embed_bias, norm_gain, w_query, w_key, w_value, w_velocity,
):
    _, rows, width, chans = feats.shape
    lat = patch_bias.shape[0]
    features, qwidth = w_query.shape
    heads = qwidth // HEAD_DIM
    tokens = rows * width // 4
    vmem = pl.BlockSpec(memory_space=pltpu.VMEM)
    anywhere = pl.BlockSpec(memory_space=pl.ANY)
    dma = pltpu.SemaphoreType.DMA
    gathered, merged, gram = pl.pallas_call(
        functools.partial(encode_kernel, n_aa, n_ba),
        out_shape=(
            jax.ShapeDtypeStruct((n_ba, n_aa * tokens, lat), BF16),
            jax.ShapeDtypeStruct((3, lat + 8, heads * SLOT), F32),
            jax.ShapeDtypeStruct((lat + 8, lat + 8), F32),
        ),
        in_specs=[anywhere, anywhere, vmem, anywhere] + [vmem] * 6 + [anywhere] * 3,
        out_specs=(vmem, vmem, vmem),
        scratch_shapes=[
            pltpu.VMEM((3, rows + 2, width, chans), BF16),
            pltpu.VMEM((3, rows + 2, width, chans), BF16),
            pltpu.VMEM((27, chans, chans), BF16),
            pltpu.VMEM((27, chans, chans), BF16),
            pltpu.VMEM((3, features, qwidth), BF16),
            pltpu.VMEM((3, rows * width, chans), F32),
            pltpu.VMEM((2, width, lat), F32),
            dma((6,)), dma((2, 8)), dma((2, 8)),
            dma((n_aa,)), dma((n_aa,)),
            dma((n_ba // 2,)), dma((n_ba // 2,)),
            dma((n_ba // 2,)), dma((n_ba // 2,)),
        ],
        compiler_params=pltpu.CompilerParams(
            collective_id=0, has_side_effects=True, vmem_limit_bytes=VMEM_BYTES
        ),
        name="encode",
    )(
        feats, conv_one.reshape(27, chans, chans), bias_one[None],
        conv_two.reshape(27, chans, chans), bias_two[None],
        patch_weight, patch_bias[None], embed_weight, embed_bias[None], norm_gain[None],
        w_query, w_key, w_value,
    )
    total = n_ba * n_aa * tokens
    span = max(tokens, min(256, n_ba * tokens))
    chunk = math.gcd(total, 1024)
    return pl.pallas_call(
        functools.partial(attend_kernel, n_aa, n_ba, span, chunk),
        out_shape=jax.ShapeDtypeStruct((tokens, lat), F32),
        in_specs=[vmem] * 4,
        out_specs=vmem,
        scratch_shapes=[
            pltpu.VMEM((heads, n_ba * tokens, SLOT), BF16),
            pltpu.VMEM((heads, total, SLOT), BF16),
            pltpu.VMEM((heads, total, SLOT), BF16),
            pltpu.VMEM((3, 2, lat, heads * SLOT), BF16),
            pltpu.VMEM((n_ba, tokens, lat), BF16),
            pltpu.VMEM((n_ba, tokens, lat), BF16),
            dma((n_ba,)), dma((n_ba,)),
        ],
        compiler_params=pltpu.CompilerParams(
            collective_id=1, has_side_effects=True, vmem_limit_bytes=VMEM_BYTES
        ),
        name="attend",
    )(gathered, merged, gram, w_velocity)


def solution(mesh):
    return jax.shard_map(
        functools.partial(on_device, mesh.shape["aa"], mesh.shape["ba"]),
        mesh=mesh,
        in_specs=(
            P("aa", "ba", None, None), P(), P(), P(), P(), P(), P(), P(), P(), P(),
            P(None, "ba"), P(None, "ba"), P(None, "ba"), P("ba", None),
        ),
        out_specs=P(("aa", "ba"), None),
        check_vma=False,
    )
```

time: 334 us -> 90.8 us (0.27)
  waiting for transfers between devices: 140 us -> 0 us
  Pallas kernels: 0 us -> 89.1 us
  matrix products: 78.4 us -> 0 us
  other arithmetic: 45.5 us -> 0 us
  starting transfers between devices: 20.9 us -> 0 us
  local copies, waits for them, and re-layouts: 19.2 us -> 1.47 us
  blocking collectives: 15 us -> 0 us
  between operations: 13.7 us -> 0.02 us
    pallas_call x0 -> x2, Pallas kernels: none -> 89.1 us  [the longest x1 44.9 us: on_device(): pl.pallas_call(functools.partial(attend_kernel, n_aa, n_ba, span, chunk),...]
    all_gather x2 -> x0, waiting for transfers between devices: 89 us -> none  [the longest x1 46.1 us: attend(): value_rows = lax.all_gather(values, 'aa', axis=0, tiled=True)]
    dot_general x30 -> x0, matrix products: 78.4 us -> none  [the longest x4 32.6 us: one_step(): jnp.einsum('qhd,khd->hqk', query_heads, key_block, preferred_element_type...]
    reduce_sum x5 -> x0, other arithmetic: 35.3 us -> none  [the longest x4 34.1 us: one_step(): denom = denom * fade + probs.sum(-1)]
    reduce_scatter x1 -> x0, waiting for transfers between devices: 32.6 us -> none  [on_device(): lax.psum_scatter(jnp.dot(attended, w_velocity, preferred_element_type=jnp...]
    ppermute x8 -> x0, starting transfers between devices: 20.5 us -> none  [the longest x4 15.2 us: with_halo(): lax.ppermute(tail, axis, [(i, (i + 1) % count) for i in range(ends)])]
    ppermute x8 -> x0, waiting for transfers between devices: 17.4 us -> none  [the longest x4 10.2 us: with_halo(): lax.ppermute(head, axis, [((i + 1) % count, i) for i in range(ends)])]
    all_gather x1 -> x0, blocking collectives: 15 us -> none  [on_device(): lax.all_gather(latents, 'ba', axis=0, tiled=True)]
  transfers between devices with their start and end apart: 11 -> 0, of which waited for: 9 -> 0; matrix products, arithmetic and copies ran while one was open for 2% -> 0% of each run, Pallas kernels for 0% -> 0%
where the time goes in v1:
time: 90.8 us; the launch traced here: 90.6 us
  Pallas kernels  89.1 us (98%)
  local copies, waits for them, and re-layouts  1.47 us (2%)
    pallas_call x1, Pallas kernels, on_device(): pl.pallas_call(functools.partial(attend_kernel, n_aa, n_ba, span, chunk),...  44.9 us
    pallas_call x1, Pallas kernels, on_device(): pl.pallas_call(functools.partial(encode_kernel, n_aa, n_ba), out_shape=(j...  44.2 us

profile of v1, /device:TPU:0, one launch (start us, length us, event | category | flops | bytes accessed | tf_op | source)
XLA Modules:
  0.0 90.6 jit_solution(14224428511626390813)
XLA Ops:
  0.0 44.2 %encode.1 = (bf16[8,512,128]{2,1,0:T(8,128)(2,1)}, f32[3,136,512]{2,1,0:T(8,128)}, f32[136,136]{1,0:T(8,128)}) custom-call(bf16[1,4,128,256]{3,2,1,0:T(8,128)(2,1)} %feats.1, bf16[27,256,256]{2,1,0:T(8,128)(2,1)} %bitcast.7, f32[1,256]{1,0:T(1,128)} %bitcast.11, bf16[27,256,256]{2,1,0:T(8,128)(2,1)} %bitcast.8, f32[1,256]{1,0:T(1,128)} %bitcast.12, ...), custom_call_target="tpu_custom_call" | custom-call | tf_op jit(solution)/shard_map/encode/pallas_call | solution.py:392
  44.2 44.9 %attend.1 = f32[128,128]{1,0:T(8,128)} custom-call(bf16[8,512,128]{2,1,0:T(8,128)(2,1)} %get-tuple-element.8.gathered, f32[3,136,512]{2,1,0:T(8,128)} %get-tuple-element.9.merged, f32[136,136]{1,0:T(8,128)} %get-tuple-element.10.gram, bf16[256,128]{1,0:T(8,128)(2,1)} %w_velocity.1), custom_call_target="tpu_custom_call" | custom-call | tf_op jit(solution)/shard_map/attend/pallas_call | solution.py:427
  89.1 1.5 %copy.16 = f32[128,128]{1,0:T(8,128)} copy(f32[128,128]{1,0:T(8,128)} %attend.1) | data formatting | bytes 131072

commit v2 on v1

v2 whole, which is shorter than its diff:
```python
import functools
import math

import jax
import jax.numpy as jnp
from jax import lax
from jax.experimental import pallas as pl
from jax.experimental.pallas import tpu as pltpu
from jax.sharding import PartitionSpec as P

HEAD_DIM = 64
SLOT = 128
MESH = pl.DeviceIdType.MESH
F32 = jnp.float32
BF16 = jnp.bfloat16
VMEM_BYTES = 67043328


def dot(left, right):
    return jnp.dot(left, right, preferred_element_type=F32)


def two_parts(value):
    high = value.astype(BF16)
    return high, (value - high.astype(F32)).astype(BF16)


def gelu(value):
    return 0.5 * value * (1.0 + lax.erf(value * (0.5**0.5)))


def whole_kernel(
    n_aa, n_ba, span, chunk,
    feats, conv_one, bias_one, conv_two, bias_two, patch_weight, patch_bias,
    embed_weight, embed_bias, norm_gain, w_query, w_key, w_value, w_velocity,
    out,
    field_one, field_two, taps, w_joined, acc, pair, gathered, split, offsets, gram_split, gram,
    queries, keys, values, shares, arrived,
    load_sem, aa_side_send, aa_side_recv, ba_side_send, ba_side_recv,
    aa_send, aa_recv, ba_send, ba_recv, core_send, core_recv, share_send, share_recv,
):
    aa, ba = lax.axis_index("aa"), lax.axis_index("ba")
    _, rows, width, chans = feats.shape
    partner = ba + 1 - 2 * (ba % 2)
    half = n_ba // 2
    heads = w_query.shape[1] // HEAD_DIM
    tokens = rows * width // 4
    lat = patch_bias.shape[1]

    def load(source, target, at):
        return pltpu.make_async_copy(source, target, load_sem.at[at])

    loads = [
        load(feats.at[0], field_one.at[1, pl.ds(1, rows)], 0),
        load(conv_one, taps, 1),
        load(w_query, w_joined.at[0], 2),
        load(w_key, w_joined.at[1], 3),
        load(w_value, w_joined.at[2], 4),
    ]
    for one in loads:
        one.start()

    def aa_there(side):
        return aa > 0 if side == -1 else aa < n_aa - 1

    def ba_there(side):
        return ba > 0 if side == -1 else ba < n_ba - 1

    barrier = pltpu.get_barrier_semaphore()
    for step in range(1, n_aa):
        pl.semaphore_signal(
            barrier, inc=1, device_id=((aa + step) % n_aa, ba), device_id_type=MESH
        )
    for step in range(1, n_ba):
        pl.semaphore_signal(
            barrier, inc=1, device_id=(aa, (ba + step) % n_ba), device_id_type=MESH
        )

    def along_time(field, side, piece):
        row = (slice(1, 2), slice(rows, rows + 1), slice(2, rows))[piece]
        at = (0 if field is field_one else 1, (side + 1) // 2, piece)
        return pltpu.make_async_remote_copy(
            src_ref=field.at[1, row], dst_ref=field.at[1 - side, row],
            send_sem=aa_side_send.at[at], recv_sem=aa_side_recv.at[at],
            device_id=(aa + side, ba), device_id_type=MESH,
        )

    def along_rows(field, frame, side):
        source, target = (rows, 0) if side == 1 else (1, rows + 1)
        at = (0 if field is field_one else 1, frame, (side + 1) // 2)
        return pltpu.make_async_remote_copy(
            src_ref=field.at[frame, pl.ds(source, 1)], dst_ref=field.at[frame, pl.ds(target, 1)],
            send_sem=ba_side_send.at[at], recv_sem=ba_side_recv.at[at],
            device_id=(aa, ba + side), device_id_type=MESH,
        )

    def send_field(field):
        for side in (-1, 1):
            pl.when(ba_there(side))(along_rows(field, 1, side).start)
        for piece in range(3):
            for side in (-1, 1):
                pl.when(aa_there(side))(along_time(field, side, piece).start)

    def take_time(field, pieces):
        for side in (-1, 1):
            @pl.when(aa_there(-side))
            def _():
                for piece in pieces:
                    along_time(field, side, piece).wait_recv()

    def relay_rows(field):
        for frame, behind in ((0, -1), (2, 1)):
            for side in (-1, 1):
                pl.when(jnp.logical_and(aa_there(behind), ba_there(side)))(
                    along_rows(field, frame, side).start
                )

    def take_rows(field, frame):
        for side in (-1, 1):
            inside = ba_there(-side)
            if frame != 1:
                inside = jnp.logical_and(inside, aa_there(frame - 1))
            pl.when(inside)(along_rows(field, frame, side).wait_recv)

    def sent(field):
        for side in (-1, 1):
            @pl.when(aa_there(side))
            def _():
                for piece in range(3):
                    along_time(field, side, piece).wait_send()

            pl.when(ba_there(side))(along_rows(field, 1, side).wait_send)
            for frame, behind in ((0, -1), (2, 1)):
                pl.when(jnp.logical_and(aa_there(behind), ba_there(side)))(
                    along_rows(field, frame, side).wait_send
                )

    def blank(field):
        line = jnp.zeros((width, chans), BF16)
        for frame, behind in ((0, -1), (2, 1)):
            @pl.when(jnp.logical_not(aa_there(behind)))
            def _():
                for row in range(rows + 2):
                    field[frame, row] = line

            @pl.when(aa_there(behind))
            def _():
                for side, row in ((-1, 0), (1, rows + 1)):
                    @pl.when(jnp.logical_not(ba_there(side)))
                    def _():
                        field[frame, row] = line
        for side, row in ((-1, 0), (1, rows + 1)):
            @pl.when(jnp.logical_not(ba_there(side)))
            def _():
                field[1, row] = line

    blank(field_one)
    blank(field_two)
    pl.semaphore_wait(barrier, n_aa - 1 + n_ba - 1)
    loads[0].wait()
    send_field(field_one)

    def merge_weights():
        embed = embed_weight[...].astype(F32)
        centred = jnp.concatenate(
            [
                embed - embed.mean(-1, keepdims=True),
                jnp.broadcast_to(
                    embed_bias[...] - embed_bias[...].mean(-1, keepdims=True),
                    (8, embed.shape[1]),
                ),
            ],
            axis=0,
        )
        gram[...] = lax.dot_general(
            centred, centred, (((1,), (1,)), ((), ())),
            precision=lax.Precision.HIGHEST, preferred_element_type=F32,
        ) * (1.0 / embed.shape[1])
        high, low = two_parts(gram[:lat, :lat])
        gram_split[:lat] = high
        gram_split[lat:] = low
        gained_high, gained_low = two_parts(centred * norm_gain[...])
        for which in range(3):
            loads[2 + which].wait()
            product = dot(gained_high, w_joined[which]) + dot(gained_low, w_joined[which])
            if which == 0:
                product = product * (HEAD_DIM**-0.5 * math.log2(math.e))
            blanks = jnp.zeros((product.shape[0], SLOT - HEAD_DIM), F32)
            for head in range(heads):
                piece = jnp.concatenate(
                    [product[:, head * HEAD_DIM : (head + 1) * HEAD_DIM], blanks], axis=1
                )
                slot = slice(head * SLOT, (head + 1) * SLOT)
                high, low = two_parts(piece[:lat])
                split[which, :lat, slot] = high
                split[which, lat:, slot] = low
                offsets[which, :, slot] = piece[lat:]

    def convolve(field, bias, filler):
        def tap(shift_t, shift_r, first):
            window = field[shift_t, pl.ds(shift_r, rows)].reshape(rows * width, chans)
            for shift_w in range(3):
                part = dot(window, taps[(shift_t * 3 + shift_r) * 3 + shift_w])
                if first:
                    acc[shift_w] = part
                else:
                    acc[shift_w] += part

        tap(1, 1, True)
        take_rows(field, 1)
        tap(1, 0, False)
        tap(1, 2, False)
        take_time(field, (0, 1))
        relay_rows(field)
        filler()
        take_time(field, (2,))
        tap(0, 1, False)
        tap(2, 1, False)
        take_rows(field, 0)
        take_rows(field, 2)

        @pl.loop(0, 2)
        def _(index):
            tap(0, 2 * index, False)
            tap(2, 2 * index, False)

        total = acc[1] + bias
        place = lax.broadcasted_iota(jnp.int32, total.shape, 0) % width
        total += jnp.where(place == 0, 0.0, pltpu.roll(acc[0], 1, 0))
        total += jnp.where(place == width - 1, 0.0, pltpu.roll(acc[2], rows * width - 1, 0))
        return total

    loads[1].wait()
    first = gelu(convolve(field_one, bias_one[...], merge_weights)).astype(BF16)
    field_two[1, 1 : rows + 1] = first.reshape(rows, width, chans)
    send_field(field_two)
    again = load(conv_two, taps, 5)
    again.start()
    again.wait()
    total = convolve(field_two, bias_two[...], lambda: None)
    own = field_two[1, 1 : rows + 1].reshape(rows * width, chans).astype(F32)
    second = (own + gelu(total)).astype(BF16)

    line = width // 2
    for block in range(rows // 2):
        upper = second[(2 * block) * width : (2 * block + 1) * width]
        lower = second[(2 * block + 1) * width : (2 * block + 2) * width]
        for col in range(2):
            pair[col] = dot(upper, patch_weight[0, col]) + dot(lower, patch_weight[1, col])
        patches = (
            pair[0, pl.ds(0, line, stride=2), :] + pair[1, pl.ds(1, line, stride=2), :]
            + patch_bias[...]
        ).astype(BF16)
        gathered[ba, pl.ds(pl.multiple_of(aa * tokens + block * line, line), line), :] = patches

    def along_aa(step):
        block = gathered.at[ba, pl.ds(pl.multiple_of(aa * tokens, tokens), tokens)]
        return pltpu.make_async_remote_copy(
            src_ref=block, dst_ref=block, send_sem=aa_send.at[step], recv_sem=aa_recv.at[step],
            device_id=((aa + step) % n_aa, ba), device_id_type=MESH,
        )

    def along_ba(step):
        return pltpu.make_async_remote_copy(
            src_ref=gathered.at[ba], dst_ref=gathered.at[ba],
            send_sem=ba_send.at[step], recv_sem=ba_recv.at[step],
            device_id=(aa, (ba + 2 * step) % n_ba), device_id_type=MESH,
        )

    def to_partner(step):
        block = gathered.at[(ba + n_ba - 2 * step) % n_ba]
        return pltpu.make_async_remote_copy(
            src_ref=block, dst_ref=block, send_sem=core_send.at[step], recv_sem=core_recv.at[step],
            device_id=(aa, partner), device_id_type=MESH,
        )

    slope = 2.0 * gram[lat : lat + 1, :lat]
    floor = gram[lat : lat + 1, lat : lat + 1]
    column = lax.broadcasted_iota(jnp.int32, (n_aa * tokens, SLOT), 1)

    def spread_of(latents, twice):
        bent = dot(twice, gram_split[...]) + slope
        power = (bent * latents.astype(F32)).sum(-1, keepdims=True) + floor
        return lax.rsqrt(jnp.maximum(power, 0.0) + 1e-05)

    def project(twice, scale, which):
        return ((dot(twice, split[which]) + offsets[which, :1]) * scale).astype(BF16)

    def take_block(block):
        latents = gathered[block]
        twice = jnp.concatenate([latents, latents], axis=1)
        scale = spread_of(latents, twice)
        projected_keys = project(twice, scale, 1)
        projected_values = project(twice, scale, 2)
        length = n_aa * tokens
        where = pl.ds(pl.multiple_of(block * length, length), length)
        for head in range(heads):
            keys[head, where] = projected_keys[:, head * SLOT : (head + 1) * SLOT]
            values[head, where] = jnp.where(
                column == HEAD_DIM,
                jnp.ones((), BF16),
                projected_values[:, head * SLOT : (head + 1) * SLOT],
            )
        mine = gathered[block, pl.ds(pl.multiple_of(aa * tokens, tokens), tokens)]
        twice = jnp.concatenate([mine, mine], axis=1)
        asked = project(twice, spread_of(mine, twice), 0)
        there = pl.ds(pl.multiple_of(block * tokens, tokens), tokens)
        for head in range(heads):
            queries[head, there] = asked[:, head * SLOT : (head + 1) * SLOT]

    for step in range(1, n_aa):
        along_aa(step).start()
    sent(field_one)
    sent(field_two)
    for step in range(1, n_aa):
        along_aa(step).wait_recv()
    for step in range(1, half):
        along_ba(step).start()
    to_partner(0).start()
    take_block(ba)
    to_partner(0).wait_recv()
    take_block(partner)

    @pl.loop(1, half)
    def _(step):
        along_ba(step).wait_recv()
        to_partner(step).start()
        take_block((ba + n_ba - 2 * step) % n_ba)

    @pl.loop(1, half)
    def _(step):
        to_partner(step).wait_recv()
        take_block((partner + n_ba - 2 * step) % n_ba)

    for step in range(1, n_aa):
        along_aa(step).wait_send()
    for step in range(1, half):
        along_ba(step).wait_send()
    for step in range(half):
        to_partner(step).wait_send()

    def share(dest):
        offset = (dest + n_ba - ba) % n_ba
        return pltpu.make_async_remote_copy(
            src_ref=shares.at[dest], dst_ref=arrived.at[ba],
            send_sem=share_send.at[offset], recv_sem=share_recv.at[offset],
            device_id=(aa, dest), device_id_type=MESH,
        )

    per_span = span // tokens
    spans = n_ba // per_span
    total = keys.shape[1]
    big = math.gcd(total, 4096)

    @pl.loop(0, spans)
    def _(step):
        at = (ba // per_span + 1 + step) % spans
        where = pl.ds(pl.multiple_of(at * span, span), span)

        def one_head(head, velocity):
            asked = queries[head, where]

            def one_big(index, state):
                best, accum = state
                for piece in range(big // chunk):
                    held = pl.ds(pl.multiple_of(index * big + piece * chunk, chunk), chunk)
                    scores = lax.dot_general(
                        asked, keys[head, held], (((1,), (1,)), ((), ())),
                        preferred_element_type=F32,
                    )
                    peak = jnp.maximum(best, scores.max(-1, keepdims=True))
                    probs = jnp.exp2(scores - peak).astype(BF16)
                    accum = accum * jnp.exp2(best - peak) + dot(probs, values[head, held])
                    best = peak
                return best, accum

            state = (jnp.full((span, 1), -jnp.inf, F32), jnp.zeros((span, SLOT), F32))
            if total == big:
                _, accum = one_big(0, state)
            else:
                _, accum = lax.fori_loop(0, total // big, one_big, state)
            attended = (accum[:, :HEAD_DIM] / accum[:, HEAD_DIM : HEAD_DIM + 1]).astype(BF16)
            rows = pl.ds(pl.multiple_of(head * HEAD_DIM, HEAD_DIM), HEAD_DIM)
            return velocity + dot(attended, w_velocity[rows])

        velocity = lax.fori_loop(0, heads, one_head, jnp.zeros((span, w_velocity.shape[1]), F32))
        for part in range(per_span):
            dest = at * per_span + part
            shares[dest] = velocity[part * tokens : (part + 1) * tokens].astype(BF16)

            @pl.when(dest != ba)
            def _():
                share(dest).start()

    summed = shares[ba].astype(F32)
    for offset in range(1, n_ba):
        share((ba + offset) % n_ba).wait_recv()
        summed += arrived[(ba + n_ba - offset) % n_ba].astype(F32)
    out[...] = summed
    for offset in range(1, n_ba):
        share((ba + offset) % n_ba).wait_send()


def on_device(
    n_aa, n_ba,
    feats, conv_one, bias_one, conv_two, bias_two, patch_weight, patch_bias,
    embed_weight, embed_bias, norm_gain, w_query, w_key, w_value, w_velocity,
):
    _, rows, width, chans = feats.shape
    lat = patch_bias.shape[0]
    features, qwidth = w_query.shape
    heads = qwidth // HEAD_DIM
    tokens = rows * width // 4
    total = n_ba * n_aa * tokens
    span = max(tokens, min(512, n_ba * tokens))
    chunk = math.gcd(total, 2048)
    vmem = pl.BlockSpec(memory_space=pltpu.VMEM)
    anywhere = pl.BlockSpec(memory_space=pl.ANY)
    dma = pltpu.SemaphoreType.DMA
    return pl.pallas_call(
        functools.partial(whole_kernel, n_aa, n_ba, span, chunk),
        out_shape=jax.ShapeDtypeStruct((tokens, lat), F32),
        in_specs=[anywhere, anywhere, vmem, anywhere] + [vmem] * 6 + [anywhere] * 3 + [vmem],
        out_specs=vmem,
        scratch_shapes=[
            pltpu.VMEM((3, rows + 2, width, chans), BF16),
            pltpu.VMEM((3, rows + 2, width, chans), BF16),
            pltpu.VMEM((27, chans, chans), BF16),
            pltpu.VMEM((3, features, qwidth), BF16),
            pltpu.VMEM((3, rows * width, chans), F32),
            pltpu.VMEM((2, width, lat), F32),
            pltpu.VMEM((n_ba, n_aa * tokens, lat), BF16),
            pltpu.VMEM((3, 2 * lat, heads * SLOT), BF16),
            pltpu.VMEM((3, 8, heads * SLOT), F32),
            pltpu.VMEM((2 * lat, lat), BF16),
            pltpu.VMEM((lat + 8, lat + 8), F32),
            pltpu.VMEM((heads, n_ba * tokens, SLOT), BF16),
            pltpu.VMEM((heads, total, SLOT), BF16),
            pltpu.VMEM((heads, total, SLOT), BF16),
            pltpu.VMEM((n_ba, tokens, lat), BF16),
            pltpu.VMEM((n_ba, tokens, lat), BF16),
            dma((6,)),
            dma((2, 2, 3)), dma((2, 2, 3)), dma((2, 3, 2)), dma((2, 3, 2)),
            dma((n_aa,)), dma((n_aa,)),
            dma((n_ba // 2,)), dma((n_ba // 2,)),
            dma((n_ba // 2,)), dma((n_ba // 2,)),
            dma((n_ba,)), dma((n_ba,)),
        ],
        compiler_params=pltpu.CompilerParams(
            collective_id=0, has_side_effects=True, vmem_limit_bytes=VMEM_BYTES
        ),
        name="whole",
    )(
        feats, conv_one.reshape(27, chans, chans), bias_one[None],
        conv_two.reshape(27, chans, chans), bias_two[None],
        patch_weight, patch_bias[None], embed_weight, embed_bias[None], norm_gain[None],
        w_query, w_key, w_value, w_velocity,
    )


def solution(mesh):
    return jax.shard_map(
        functools.partial(on_device, mesh.shape["aa"], mesh.shape["ba"]),
        mesh=mesh,
        in_specs=(
            P("aa", "ba", None, None), P(), P(), P(), P(), P(), P(), P(), P(), P(),
            P(None, "ba"), P(None, "ba"), P(None, "ba"), P("ba", None),
        ),
        out_specs=P(("aa", "ba"), None),
        check_vma=False,
    )
```

time: 90.8 us -> 72.9 us (0.80)
  Pallas kernels: 89.1 us -> 71.2 us
    pallas_call x2 -> x1, Pallas kernels: 89.1 us -> 71.2 us  [on_device(): pl.pallas_call(functools.partial(whole_kernel, n_aa, n_ba, span, chunk),...]
where the time goes in v2:
time: 72.9 us; the launch traced here: 72.7 us
  Pallas kernels  71.2 us (98%)
  local copies, waits for them, and re-layouts  1.47 us (2%)
    pallas_call x1, Pallas kernels, on_device(): pl.pallas_call(functools.partial(whole_kernel, n_aa, n_ba, span, chunk),...  71.2 us
    unnamed x1, local copies, waits for them, and re-layouts  1.47 us

profile of v2, /device:TPU:0, one launch (start us, length us, event | category | flops | bytes accessed | tf_op | source)
XLA Modules:
  0.0 72.7 jit_solution(2489680248494101148)
XLA Ops:
  0.0 71.2 %whole.1 = f32[128,128]{1,0:T(8,128)} custom-call(bf16[1,4,128,256]{3,2,1,0:T(8,128)(2,1)} %feats.1, bf16[27,256,256]{2,1,0:T(8,128)(2,1)} %bitcast.7, f32[1,256]{1,0:T(1,128)} %bitcast.11, bf16[27,256,256]{2,1,0:T(8,128)(2,1)} %bitcast.8, f32[1,256]{1,0:T(1,128)} %bitcast.12, bf16[2,2,256,128]{3,2,1,0:T(8,128)(2,1)} %patch_weight.1, f32[1,128]{1,0:T(1,128)} %bitcast.13, ...), custom_call_target="tpu_custom_call" | custom-call | tf_op jit(solution)/shard_map/whole/pallas_call | solution.py:420
  71.2 1.5 %copy.16 = f32[128,128]{1,0:T(8,128)} copy(f32[128,128]{1,0:T(8,128)} %whole.1) | data formatting | bytes 131072

commit v3 on v2

--- a/solution.py
+++ b/solution.py
@@ -383,7 +383,7 @@
             rows = pl.ds(pl.multiple_of(head * HEAD_DIM, HEAD_DIM), HEAD_DIM)
             return velocity + dot(attended, w_velocity[rows])
 
-        velocity = lax.fori_loop(0, heads, one_head, jnp.zeros((span, w_velocity.shape[1]), F32))
+        velocity = lax.fori_loop(0, heads, one_head, jnp.zeros((span, w_velocity.shape[1]), F32), unroll=2)
         for part in range(per_span):
             dest = at * per_span + part
             shares[dest] = velocity[part * tokens : (part + 1) * tokens].astype(BF16)

time: 72.9 us -> 72.3 us (level)
  no operation moved by 1% of the time
where the time goes in v3:
time: 72.3 us; the launch traced here: 72 us
  Pallas kernels  70.6 us (98%)
  local copies, waits for them, and re-layouts  1.47 us (2%)
    pallas_call x1, Pallas kernels, on_device(): pl.pallas_call(functools.partial(whole_kernel, n_aa, n_ba, span, chunk),...  70.6 us
    unnamed x1, local copies, waits for them, and re-layouts  1.47 us

profile of v3, /device:TPU:0, one launch (start us, length us, event | category | flops | bytes accessed | tf_op | source)
XLA Modules:
  0.0 72.0 jit_solution(16284078765233630472)
XLA Ops:
  0.0 70.6 %whole.1 = f32[128,128]{1,0:T(8,128)} custom-call(bf16[1,4,128,256]{3,2,1,0:T(8,128)(2,1)} %feats.1, bf16[27,256,256]{2,1,0:T(8,128)(2,1)} %bitcast.7, f32[1,256]{1,0:T(1,128)} %bitcast.11, bf16[27,256,256]{2,1,0:T(8,128)(2,1)} %bitcast.8, f32[1,256]{1,0:T(1,128)} %bitcast.12, bf16[2,2,256,128]{3,2,1,0:T(8,128)(2,1)} %patch_weight.1, f32[1,128]{1,0:T(1,128)} %bitcast.13, ...), custom_call_target="tpu_custom_call" | custom-call | tf_op jit(solution)/shard_map/whole/pallas_call | solution.py:420
  70.6 1.5 %copy.16 = f32[128,128]{1,0:T(8,128)} copy(f32[128,128]{1,0:T(8,128)} %whole.1) | data formatting | bytes 131072
